TPU v7x, 32 devices: a whole 2x2x4 slice. The times are simulated.
32 devices in a mesh: groups: 2 (over y), frames: 4 (over z), fsdp: 2 (over x), heads: 2 (over core).
Axes of the slice: x: 2, y: 2, z: 4, core: 2. Of those that a mesh axis runs over, the one named last changes fastest.
Arguments:
- frames_in: bfloat16 [4, 768, 1536], P(('groups', 'fsdp'), 'frames', 'heads'), parts along dimension 0, may hold values from -6 to 6
- lengths: int32 [4], P(('groups', 'fsdp')), parts along dimension 0, may hold values from 192 to 768, as said below
- w_query: bfloat16 [1536, 768], P(('frames', 'fsdp'), 'heads')
- w_key: bfloat16 [1536, 768], P(('frames', 'fsdp'), 'heads'), may hold values from -0.15625 to 0.15625
- w_value: bfloat16 [1536, 768], P(('frames', 'fsdp'), 'heads'), may hold values from -0.15625 to 0.15625
- w_out: bfloat16 [768, 1536], P('heads', ('frames', 'fsdp')), may hold values from -0.21875 to 0.21875
- w_glu: bfloat16 [1536, 2, 1536], P('fsdp', None, 'heads'), may hold values from -0.15625 to 0.15625
- dw_kernel: bfloat16 [31, 1536], P(None, 'heads'), may hold values from -1 to 1
- w_pw: bfloat16 [1536, 1536], P('heads', 'fsdp'), may hold values from -0.15625 to 0.15625
Outputs:
- block_out: bfloat16 [4, 768, 1536], P(('groups', 'fsdp'), 'frames', 'heads'), parts along dimension 0
There are 2 independent parts, one for each index of `groups`. A program takes and returns all parts, laid end to end along the dimension named above; an argument that names none is the same for every part. Nothing has to cross between parts.
Inputs may be any that keep to these rules, and one draw needn't show every extreme that they name: `lengths`: each utterance counts at least 192 valid frames, and in every group some utterance is valid over all 768 frames.
All inputs are finite; a program needn't handle non-finite values.
Results may differ from a plain program's by a relative error of at most 0.012.
The roundings to bfloat16 on the way count: a program that leaves them out, or rounds other values in their place, can miss the bound.
Values may be sent and summed in bfloat16 or wider, within the bound.
No kernel may reach another device: no remote copies, remote signals or barrier semaphores. Data moves between devices by JAX's collectives and lax.ppermute only.
A program may use at most 64 MiB of HBM per device.

v0:
```python
import math
import jax
import jax.numpy as jnp
from jax import lax
from jax.sharding import PartitionSpec as P

HEAD_DIM = 96
KERNEL = 31
EPS = 1e-05
NEG_FILL = -1e30


def padded_2(cells, sides, width):
    for axis, dim in sides:
        count = lax.axis_size(axis)
        ends = count - 1
        head = lax.slice_in_dim(cells, 0, width, axis=dim)
        tail = lax.slice_in_dim(cells, cells.shape[dim] - width, cells.shape[dim], axis=dim)
        cells = jnp.concatenate(
            [
                lax.ppermute(tail, axis, [(i, (i + 1) % count) for i in range(ends)]),
                cells,
                lax.ppermute(head, axis, [((i + 1) % count, i) for i in range(ends)]),
            ],
            axis=dim,
        )
    return cells


def layer_norm(rows):
    values = rows.astype(jnp.float32)
    mean_row = jnp.mean(values, axis=-1, keepdims=True)
    centred = values - mean_row
    variance = jnp.mean(centred * centred, axis=-1, keepdims=True)
    return centred * lax.rsqrt(variance + EPS)


def shards(frames_in, lengths, w_query, w_key, w_value, w_out, w_glu, dw_kernel, w_pw):
    full_rows = lax.all_gather(frames_in, "heads", axis=2, tiled=True)[0]
    frame_count = full_rows.shape[0]
    half_width = frames_in.shape[2]
    own_start = lax.axis_index("heads") * half_width
    normed = layer_norm(full_rows).astype(jnp.bfloat16)
    att_cols = w_query.shape[1]
    pieces = (
        lax.all_gather(w_query, ("frames", "fsdp"), axis=0, tiled=True),
        lax.all_gather(w_key, ("frames", "fsdp"), axis=0, tiled=True),
        lax.all_gather(w_value, ("frames", "fsdp"), axis=0, tiled=True),
    )
    sliced = normed
    projected = tuple(
        (jnp.dot(sliced, piece_part, preferred_element_type=jnp.float32) for piece_part in pieces)
    )
    head_count = att_cols // HEAD_DIM
    queries = projected[0].astype(jnp.bfloat16).reshape(frame_count, head_count, HEAD_DIM)
    key_rows = projected[1].astype(jnp.bfloat16)
    value_rows = projected[2].astype(jnp.bfloat16)
    length = lengths[0]
    scale_factor = 1.0 / math.sqrt(HEAD_DIM)
    start_max = jnp.full((frame_count, head_count), NEG_FILL, jnp.float32)
    pieces = (
        lax.all_gather(key_rows, "frames", axis=0, tiled=True),
        lax.all_gather(value_rows, "frames", axis=0, tiled=True),
    )
    key_block = pieces[0].reshape(-1, head_count, HEAD_DIM)
    value_block = pieces[1].reshape(-1, head_count, HEAD_DIM)
    block_rows = key_block.shape[0]
    scores = (
        jnp.einsum("qhd,khd->qhk", queries, key_block, preferred_element_type=jnp.float32)
        * scale_factor
    )
    valid = jnp.arange(block_rows, dtype=jnp.int32) < length
    masked = jnp.where(valid, scores, NEG_FILL)
    new_max = jnp.maximum(start_max, jnp.max(masked, axis=2))
    expo = jnp.where(valid, jnp.exp(masked - new_max[:, :, None]), 0.0)
    new_sum = jnp.sum(expo, axis=2)
    block_acc = jnp.einsum(
        "qhk,khd->qhd", expo.astype(jnp.bfloat16), value_block, preferred_element_type=jnp.float32
    )
    context = (block_acc / new_sum[:, :, None]).reshape(frame_count, att_cols).astype(jnp.bfloat16)
    partial_value = jnp.dot(
        context,
        lax.all_gather(w_out, ("frames", "fsdp"), axis=1, tiled=True),
        preferred_element_type=jnp.float32,
    )
    total = lax.psum(partial_value.astype(jnp.bfloat16), "heads").astype(jnp.float32)
    stream_full = (full_rows.astype(jnp.float32) + total).astype(jnp.bfloat16)
    stream_own = lax.dynamic_slice_in_dim(stream_full, own_start, half_width, 1)
    normed_two = layer_norm(stream_full).astype(jnp.bfloat16)
    channels = w_glu.shape[2]
    sliced = normed_two
    glu_pre = jnp.einsum(
        "td,dgc->tgc",
        sliced,
        lax.all_gather(w_glu, "fsdp", axis=0, tiled=True),
        preferred_element_type=jnp.float32,
    )
    positions = lax.axis_index("frames") * frame_count + jnp.arange(frame_count, dtype=jnp.int32)
    live = positions < length
    gated = jnp.where(
        live[:, None], glu_pre[:, 0, :] * jax.nn.sigmoid(glu_pre[:, 1, :]), 0.0
    ).astype(jnp.bfloat16)
    padded = padded_2(gated, (("frames", 0),), KERNEL // 2)
    depth = jnp.zeros((frame_count, channels), jnp.float32)
    for tap_index in range(KERNEL):
        depth = depth + padded[tap_index : tap_index + frame_count].astype(jnp.float32) * dw_kernel[
            tap_index
        ].astype(jnp.float32)
    hidden = (depth * jax.nn.sigmoid(depth)).astype(jnp.bfloat16)
    conv_part = jnp.dot(
        hidden, lax.all_gather(w_pw, "fsdp", axis=1, tiled=True), preferred_element_type=jnp.float32
    )
    conv_half = lax.psum_scatter(
        conv_part.astype(jnp.bfloat16), "heads", scatter_dimension=1, tiled=True
    ).astype(jnp.float32)
    result = (stream_own.astype(jnp.float32) + conv_half).astype(jnp.bfloat16)
    return result[None]


def solution(mesh):
    in_specs = (
        P(("groups", "fsdp"), "frames", "heads"),
        P(("groups", "fsdp")),
        P(("frames", "fsdp"), "heads"),
        P(("frames", "fsdp"), "heads"),
        P(("frames", "fsdp"), "heads"),
        P("heads", ("frames", "fsdp")),
        P("fsdp", None, "heads"),
        P(None, "heads"),
        P("heads", "fsdp"),
    )
    out_specs = P(("groups", "fsdp"), "frames", "heads")
    return jax.shard_map(shards, mesh=mesh, in_specs=in_specs, out_specs=out_specs, check_vma=False)
```

profile of v0, /device:TPU:0, one launch (start us, length us, event | category | flops | bytes accessed | tf_op | source)
XLA Modules:
  0.0 307.6 jit_solution(13441506892905612474)
XLA Ops:
  7.4 0.7 all-gather.9.cloned.1.call-update
  8.1 0.7 all-gather.11.cloned.1.call-update
  8.9 0.7 all-gather.7.cloned.1.call-update
  9.6 0.5 all-gather.13.cloned.1.call-update
  10.2 2.6 all_gather.27
  12.9 0.3 fusion.13
  13.9 40.3 %all-gather.9.cloned.1.call-done = bf16[1536,384]{1,0:T(8,128)(2,1)} async-done(((bf16[192,384]{1,0:T(8,128)(2,1)}), bf16[1536,384]{1,0:T(8,128)(2,1)}) %all-gather.9.cloned.1.call-update) | async-done | bytes 1179664 | tf_op jit(solution)/shard_map/all_gather | solution.py:47
  54.2 1.8 convolution_convert_fusion.3
  56.0 18.1 %all_gather.31 = bf16[768,384]{1,0:T(8,128)(2,1)S(1)} all-gather(bf16[192,384]{1,0:T(8,128)(2,1)S(1)} %convolution_convert_fusion.3), channel_id=1, replica_groups=mesh['groups'=2,'frames'=4,'fsdp'=2,'heads'=2] {'frames'}, dimensions={0}, use_global_device_ids=true | all-gather | bytes 737280 | tf_op jit(solution)/shard_map/all_gather | solution.py:62
  74.4 22.4 %all-gather.11.cloned.1.call-done = bf16[1536,384]{1,0:T(8,128)(2,1)} async-done(((bf16[192,384]{1,0:T(8,128)(2,1)}), bf16[1536,384]{1,0:T(8,128)(2,1)}) %all-gather.11.cloned.1.call-update) | async-done | bytes 1179664 | tf_op jit(solution)/shard_map/all_gather | solution.py:46
  96.8 1.8 convolution_convert_fusion.2
  98.7 40.1 %all-gather.7.cloned.1.call-done = bf16[1536,384]{1,0:T(8,128)(2,1)} async-done(((bf16[192,384]{1,0:T(8,128)(2,1)}), bf16[1536,384]{1,0:T(8,128)(2,1)}) %all-gather.7.cloned.1.call-update) | async-done | bytes 1179664 | tf_op jit(solution)/shard_map/all_gather | solution.py:48
  138.8 1.8 convolution_convert_fusion.4
  140.6 18.1 %all_gather.29 = bf16[768,384]{1,0:T(8,128)(2,1)S(1)} all-gather(bf16[192,384]{1,0:T(8,128)(2,1)S(1)} %convolution_convert_fusion.4), channel_id=1, replica_groups=mesh['groups'=2,'frames'=4,'fsdp'=2,'heads'=2] {'frames'}, dimensions={0}, use_global_device_ids=true | all-gather | bytes 737280 | tf_op jit(solution)/shard_map/all_gather | solution.py:63
  158.9 0.6 bitcast_reduce_fusion
  159.5 0.7 fusion.2
  160.2 0.8 fusion.22
  161.0 20.3 %all-gather.13.cloned.1.call-done = bf16[384,1536]{0,1:T(8,128)(2,1)} async-done(((bf16[384,192]{0,1:T(8,128)(2,1)}), bf16[384,1536]{0,1:T(8,128)(2,1)}) %all-gather.13.cloned.1.call-update) | async-done | bytes 1179664 | tf_op jit(solution)/shard_map/all_gather | solution.py:83
  181.4 2.8 convolution_convert_fusion.1
  184.3 1.8 copy.17
  186.1 0.5 all-gather.17.cloned.1.call-update
  187.1 14.7 %all-reduce.2.cloned.1.call-done = bf16[192,1536]{1,0:T(8,128)(2,1)} async-done(((bf16[192,1536]{1,0:T(8,128)(2,1)}), bf16[192,1536]{1,0:T(8,128)(2,1)}) %all-reduce.2.cloned.1.call-update) | async-done | bytes 589840 | tf_op jit(solution)/shard_map/psum | solution.py:86
  201.8 1.3 convert_reduce_fusion
  203.1 0.3 fusion.11
  203.4 44.1 %all-gather.15.cloned.1.call-done = bf16[1536,2,768]{2,0,1:T(8,128)(2,1)} async-done(((bf16[768,2,768]{2,0,1:T(8,128)(2,1)}), bf16[1536,2,768]{2,0,1:T(8,128)(2,1)}) %all-gather.15.cloned.1.call-update) | async-done | bytes 4718608 | tf_op jit(solution)/shard_map/all_gather | solution.py:95
  247.5 3.5 %fusion.26 = f32[192,2,768]{2,0,1:T(8,128)S(1)} fusion(bf16[1536,2,768]{2,0,1:T(8,128)(2,1)} %all-gather.15.cloned.1.call-done, bf16[192,1536]{1,0:T(8,128)(2,1)S(1)} %get-tuple-element.37, f32[192]{0:T(256)S(1)} %add_rsqrt_fusion, f32[192]{0:T(256)S(1)} %broadcast_multiply_fusion), kind=kOutput, calls=%fused_computation.64 | convolution fusion | flops 907149312 | bytes 6489600 | tf_op jit(solution)/shard_map/td,dgc->tgc/dot_general | solution.py:92
  251.2 3.4 %collective-permute-start = (bf16[15,768]{1,0:T(8,128)(2,1)S(1)}, bf16[15,768]{1,0:T(8,128)(2,1)S(1)}, u32[]{:S(2)}, u32[]{:S(2)}) collective-permute-start(bf16[15,768]{1,0:T(8,128)(2,1)S(1)} %get-tuple-element.38), channel_id=1, source_target_pairs={{0,4},{4,8},{8,12},{1,5},{5,9},{9,13},{2,6},{6,10},{10,14},{3,7},{... | collective-permute-start | bytes 69128 | tf_op jit(solution)/shard_map/ppermute | solution.py:21
  254.6 1.3 collective-permute-start.1
  256.0 28.9 %all-gather.17.cloned.1.call-done = bf16[768,1536]{1,0:T(8,128)(2,1)} async-done(((bf16[768,768]{1,0:T(8,128)(2,1)}), bf16[768,1536]{1,0:T(8,128)(2,1)}) %all-gather.17.cloned.1.call-update) | async-done | bytes 2359312 | tf_op jit(solution)/shard_map/all_gather | solution.py:111
  284.8 5.5 %convolution_convert_fusion = bf16[192,1536]{1,0:T(8,128)(2,1)} fusion(bf16[768,1536]{1,0:T(8,128)(2,1)} %all-gather.17.cloned.1.call-done, bf16[192,768]{1,0:T(8,128)(2,1)S(1)} %fusion.36, bf16[15,768]{1,0:T(8,128)(2,1)S(1)} %collective-permute-done.1, bf16[15,768]{1,0:T(8,128)(2,1)S(1)} %collective-permute-done, f32[768]{0:T(1024)S(1)} %get-tuple-element.34, ...), kind=kOutput, calls=%fused_computation | convolution fusion | flops 480854016 | bytes 3385344 | tf_op jit(solution)/shard_map/dot_general | solution.py:110
  290.3 8.1 %reduce-scatter.2.cloned.1.call-done = bf16[192,768]{1,0:T(8,128)(2,1)} async-done(((bf16[192,1536]{1,0:T(8,128)(2,1)}), bf16[192,768]{1,0:T(8,128)(2,1)}) %reduce-scatter.2.cloned.1.call-update) | async-done | bytes 294928 | tf_op jit(solution)/shard_map/reduce_scatter | solution.py:113
  298.5 1.7 fusion.37
  (32 shorter events, 1.8 us)
Async XLA Ops:
  7.4 46.9 %all-gather.9.cloned.1.call-start = ((), (), s32[]{:S(2)}) async-start(), calls=%async_computation.2 | async-start | bytes 1327104 | tf_op jit(solution)/shard_map/all_gather | solution.py:47
  8.1 88.7 %all-gather.11.cloned.1.call-start = ((), (), s32[]{:S(2)}) async-start(), calls=%async_computation.3 | async-start | bytes 1327104 | tf_op jit(solution)/shard_map/all_gather | solution.py:46
  8.8 130.0 %all-gather.7.cloned.1.call-start = ((), (), s32[]{:S(2)}) async-start(), calls=%async_computation.1 | async-start | bytes 1327104 | tf_op jit(solution)/shard_map/all_gather | solution.py:48
  9.6 171.8 %all-gather.13.cloned.1.call-start = ((), (), s32[]{:S(2)}) async-start(), calls=%async_computation.4 | async-start | bytes 1327104 | tf_op jit(solution)/shard_map/all_gather | solution.py:83
  10.1 191.6 %all-reduce.2.cloned.1.call-start = ((), (), s32[]{:S(2)}) async-start(), calls=%async_computation.5 | async-start | bytes 1179648 | tf_op jit(solution)/shard_map/psum | solution.py:86
  181.4 2.9 copy-start
  184.2 63.2 %all-gather.15.cloned.1.call-start = ((), (), s32[]{:S(2)}) async-start(), calls=%async_computation.6 | async-start | bytes 7077888 | tf_op jit(solution)/shard_map/all_gather | solution.py:95
  186.1 0.8 copy-start.1
  186.1 98.7 %all-gather.17.cloned.1.call-start = ((), (), s32[]{:S(2)}) async-start(), calls=%async_computation.7 | async-start | bytes 3538944 | tf_op jit(solution)/shard_map/all_gather | solution.py:111
  186.7 111.8 %reduce-scatter.2.cloned.1.call-start = ((), (), s32[]{:S(2)}) async-start(), calls=%async_computation.8 | async-start | bytes 884736 | tf_op jit(solution)/shard_map/reduce_scatter | solution.py:113
  251.2 33.7 %collective-permute-start = (bf16[15,768]{1,0:T(8,128)(2,1)S(1)}, bf16[15,768]{1,0:T(8,128)(2,1)S(1)}, u32[]{:S(2)}, u32[]{:S(2)}) collective-permute-start(bf16[15,768]{1,0:T(8,128)(2,1)S(1)} %get-tuple-element.38), channel_id=1, source_target_pairs={{0,4},{4,8},{8,12},{1,5},{5,9},{9,13},{2,6},{6,10},{10,14},{3,7},{... | collective-permute-start | bytes 69128 | tf_op jit(solution)/shard_map/ppermute | solution.py:21
  254.6 30.3 %collective-permute-start.1 = (bf16[15,768]{1,0:T(8,128)(2,1)S(1)}, bf16[15,768]{1,0:T(8,128)(2,1)S(1)}, u32[]{:S(2)}, u32[]{:S(2)}) collective-permute-start(bf16[15,768]{1,0:T(8,128)(2,1)S(1)} %get-tuple-element.39), channel_id=1, source_target_pairs={{4,0},{8,4},{12,8},{5,1},{9,5},{13,9},{6,2},{10,6},{14,10},{7,3},{... | collective-permute-start | bytes 69128 | tf_op jit(solution)/shard_map/ppermute | solution.py:23
Sparse Core Ops, SparseCore 0:
  10.3 43.8 all-gather.8
  56.4 40.3 all-gather.10
  99.0 39.8 all-gather.6
  140.9 40.4 all-gather.12
  184.4 17.3 all-reduce.1
  290.5 7.9 reduce-scatter.1
Sparse Core Ops, SparseCore 1:
  186.3 61.2 all-gather.14
  248.9 35.9 all-gather.16
where the time goes:
time: 308 us
  waiting for transfers between devices  222 us (72%)
  blocking collectives  38.7 us (13%)
  matrix products  18.5 us (6%)
  between operations  15.7 us (5%)
  other arithmetic  5.05 us (2%)
  starting transfers between devices  4.97 us (2%)
    all_gather x1, waiting for transfers between devices, shards(): lax.all_gather(w_glu, 'fsdp', axis=0, tiled=True)  44.1 us
    all_gather x1, waiting for transfers between devices, shards(): lax.all_gather(w_key, ('frames', 'fsdp'), axis=0, tiled=True)  40.3 us
    all_gather x1, waiting for transfers between devices, shards(): lax.all_gather(w_value, ('frames', 'fsdp'), axis=0, tiled=True)  40.1 us
    all_gather x1, waiting for transfers between devices, shards(): lax.all_gather(w_pw, 'fsdp', axis=1, tiled=True)  28.9 us
    all_gather x1, waiting for transfers between devices, shards(): lax.all_gather(w_query, ('frames', 'fsdp'), axis=0, tiled=True)  22.4 us
    all_gather x1, waiting for transfers between devices, shards(): lax.all_gather(w_out, ('frames', 'fsdp'), axis=1, tiled=True)  20.3 us
    all_gather x1, blocking collectives, shards(): lax.all_gather(key_rows, 'frames', axis=0, tiled=True)  18.1 us
    all_gather x1, blocking collectives, shards(): lax.all_gather(value_rows, 'frames', axis=0, tiled=True)  18.1 us
  transfers between devices with their start and end apart: 10, of which 8 were waited for; matrix products, arithmetic and copies ran while one was open for 5% of the time, Pallas kernels for 0%

commit v1 on v0

--- a/solution.py
+++ b/solution.py
@@ -8,6 +8,17 @@
 KERNEL = 31
 EPS = 1e-05
 NEG_FILL = -1e30
+
+
+def ring_gather(x, axis, dim):
+    ways = lax.axis_size(axis)
+    pieces = [x]
+    for far in range(1, ways):
+        pieces.append(
+            lax.ppermute(pieces[far - 1], axis, [(d, (d - 1) % ways) for d in range(ways)])
+        )
+    line = jnp.concatenate(pieces, axis=dim)
+    return jnp.roll(line, lax.axis_index(axis) * x.shape[dim], axis=dim)
 
 
 def padded_2(cells, sides, width):
@@ -79,9 +90,7 @@
     )
     context = (block_acc / new_sum[:, :, None]).reshape(frame_count, att_cols).astype(jnp.bfloat16)
     partial_value = jnp.dot(
-        context,
-        lax.all_gather(w_out, ("frames", "fsdp"), axis=1, tiled=True),
-        preferred_element_type=jnp.float32,
+        context, ring_gather(w_out, ("frames", "fsdp"), 1), preferred_element_type=jnp.float32
     )
     total = lax.psum(partial_value.astype(jnp.bfloat16), "heads").astype(jnp.float32)
     stream_full = (full_rows.astype(jnp.float32) + total).astype(jnp.bfloat16)

time: 308 us -> 294 us (0.955)
  waiting for transfers between devices: 222 us -> 159 us
  starting transfers between devices: 4.97 us -> 42.1 us
  local copies, waits for them, and re-layouts: 2.57 us -> 15.2 us
    all_gather x1, waiting for transfers between devices: 40.3 us -> 0.01 us  [shards(): lax.all_gather(w_key, ('frames', 'fsdp'), axis=0, tiled=True)]
    ppermute x0 -> x7, starting transfers between devices: none -> 37 us  [ring_gather(): lax.ppermute(pieces[far - 1], axis, [(d, (d - 1) % ways) for d in range(w...]
    all_gather x1 -> x0, waiting for transfers between devices: 20.3 us -> none  [shards(): lax.all_gather(w_out, ('frames', 'fsdp'), axis=1, tiled=True)]
    ppermute x0 -> x7, waiting for transfers between devices: none -> 18.9 us  [ring_gather(): lax.ppermute(pieces[far - 1], axis, [(d, (d - 1) % ways) for d in range(w...]
    all_gather x1, waiting for transfers between devices: 22.4 us -> 3.85 us  [shards(): lax.all_gather(w_query, ('frames', 'fsdp'), axis=0, tiled=True)]
    unnamed x5 -> x24, local copies, waits for them, and re-layouts: 1.9 us -> 12.3 us
  transfers between devices with their start and end apart: 10 -> 16, of which waited for: 8 -> 13; matrix products, arithmetic and copies ran while one was open for 5% -> 8% of each run, Pallas kernels for 0% -> 0%
where the time goes in v1:
time: 294 us; the launch traced here: 293 us
  waiting for transfers between devices  159 us (54%)
  starting transfers between devices  42.1 us (14%)
  blocking collectives  36.5 us (12%)
  matrix products  19.4 us (7%)
  between operations  15.4 us (5%)
  local copies, waits for them, and re-layouts  15.2 us (5%)
  other arithmetic  5.02 us (2%)
    all_gather x1, waiting for transfers between devices, shards(): lax.all_gather(w_glu, 'fsdp', axis=0, tiled=True)  44.1 us
    all_gather x1, waiting for transfers between devices, shards(): lax.all_gather(w_value, ('frames', 'fsdp'), axis=0, tiled=True)  38.9 us
    ppermute x7, starting transfers between devices, ring_gather(): lax.ppermute(pieces[far - 1], axis, [(d, (d - 1) % ways) for d in range(w...  37 us
    all_gather x1, waiting for transfers between devices, shards(): lax.all_gather(w_pw, 'fsdp', axis=1, tiled=True)  28.7 us
    ppermute x7, waiting for transfers between devices, ring_gather(): lax.ppermute(pieces[far - 1], axis, [(d, (d - 1) % ways) for d in range(w...  18.9 us
    all_gather x1, blocking collectives, shards(): lax.all_gather(key_rows, 'frames', axis=0, tiled=True)  17.8 us
    all_gather x1, blocking collectives, shards(): lax.all_gather(value_rows, 'frames', axis=0, tiled=True)  16.3 us
    psum x1, waiting for transfers between devices, shards(): lax.psum(partial_value.astype(jnp.bfloat16), 'heads').astype(jnp.float32)  15 us
  transfers between devices with their start and end apart: 16, of which 13 were waited for; matrix products, arithmetic and copies ran while one was open for 8% of the time, Pallas kernels for 0%

profile of v1, /device:TPU:0, one launch (start us, length us, event | category | flops | bytes accessed | tf_op | source)
XLA Modules:
  0.0 293.1 jit_solution(13743615551415547358)
XLA Ops:
  8.9 6.1 %collective-permute-start = (bf16[384,192]{0,1:T(8,128)(2,1)}, bf16[384,192]{0,1:T(8,128)(2,1)S(1)}, u32[]{:S(2)}, u32[]{:S(2)}) collective-permute-start(bf16[384,192]{0,1:T(8,128)(2,1)} %param.14), channel_id=1, source_target_pairs={{0,14},{2,0},{4,2},{6,4},{8,6},{10,8},{12,10},{14,12},{1,15},{3,1}... | collective-permute-start | bytes 442376 | tf_op jit(solution)/shard_map/ppermute | solution.py:18
  15.0 2.4 all_gather.24
  18.4 5.1 %collective-permute-start.1 = (bf16[384,192]{0,1:T(8,128)(2,1)S(1)}, bf16[384,192]{0,1:T(8,128)(2,1)S(1)}, u32[]{:S(2)}, u32[]{:S(2)}) collective-permute-start(bf16[384,192]{0,1:T(8,128)(2,1)S(1)} %collective-permute-done), channel_id=1, source_target_pairs={{0,14},{2,0},{4,2},{6,4},{8,6},{10,8},{12,10},{14,12},{1,15},{3,1}... | collective-permute-start | bytes 442376 | tf_op jit(solution)/shard_map/ppermute | solution.py:18
  23.7 4.1 %collective-permute-done.1 = bf16[384,192]{0,1:T(8,128)(2,1)S(1)} collective-permute-done((bf16[384,192]{0,1:T(8,128)(2,1)S(1)}, bf16[384,192]{0,1:T(8,128)(2,1)S(1)}, u32[]{:S(2)}, u32[]{:S(2)}) %collective-permute-start.1) | collective-permute-done | bytes 147488 | tf_op jit(solution)/shard_map/ppermute | solution.py:18
  27.9 5.2 %collective-permute-start.2 = (bf16[384,192]{0,1:T(8,128)(2,1)S(1)}, bf16[384,192]{0,1:T(8,128)(2,1)S(1)}, u32[]{:S(2)}, u32[]{:S(2)}) collective-permute-start(bf16[384,192]{0,1:T(8,128)(2,1)S(1)} %collective-permute-done.1), channel_id=1, source_target_pairs={{0,14},{2,0},{4,2},{6,4},{8,6},{10,8},{12,10},{14,12},{1,15},{3,1}... | collective-permute-start | bytes 442376 | tf_op jit(solution)/shard_map/ppermute | solution.py:18
  33.1 2.7 collective-permute-done.2
  35.7 5.2 %collective-permute-start.3 = (bf16[384,192]{0,1:T(8,128)(2,1)S(1)}, bf16[384,192]{0,1:T(8,128)(2,1)S(1)}, u32[]{:S(2)}, u32[]{:S(2)}) collective-permute-start(bf16[384,192]{0,1:T(8,128)(2,1)S(1)} %collective-permute-done.2), channel_id=1, source_target_pairs={{0,14},{2,0},{4,2},{6,4},{8,6},{10,8},{12,10},{14,12},{1,15},{3,1}... | collective-permute-start | bytes 442376 | tf_op jit(solution)/shard_map/ppermute | solution.py:18
  41.6 4.9 %collective-permute-done.3 = bf16[384,192]{0,1:T(8,128)(2,1)S(1)} collective-permute-done((bf16[384,192]{0,1:T(8,128)(2,1)S(1)}, bf16[384,192]{0,1:T(8,128)(2,1)S(1)}, u32[]{:S(2)}, u32[]{:S(2)}) %collective-permute-start.3) | collective-permute-done | bytes 147488 | tf_op jit(solution)/shard_map/ppermute | solution.py:18
  46.5 5.2 %collective-permute-start.4 = (bf16[384,192]{0,1:T(8,128)(2,1)S(1)}, bf16[384,192]{0,1:T(8,128)(2,1)S(1)}, u32[]{:S(2)}, u32[]{:S(2)}) collective-permute-start(bf16[384,192]{0,1:T(8,128)(2,1)S(1)} %collective-permute-done.3), channel_id=1, source_target_pairs={{0,14},{2,0},{4,2},{6,4},{8,6},{10,8},{12,10},{14,12},{1,15},{3,1}... | collective-permute-start | bytes 442376 | tf_op jit(solution)/shard_map/ppermute | solution.py:18
  53.1 3.5 %collective-permute-done.4 = bf16[384,192]{0,1:T(8,128)(2,1)S(1)} collective-permute-done((bf16[384,192]{0,1:T(8,128)(2,1)S(1)}, bf16[384,192]{0,1:T(8,128)(2,1)S(1)}, u32[]{:S(2)}, u32[]{:S(2)}) %collective-permute-start.4) | collective-permute-done | bytes 147488 | tf_op jit(solution)/shard_map/ppermute | solution.py:18
  56.5 5.2 %collective-permute-start.5 = (bf16[384,192]{0,1:T(8,128)(2,1)S(1)}, bf16[384,192]{0,1:T(8,128)(2,1)S(1)}, u32[]{:S(2)}, u32[]{:S(2)}) collective-permute-start(bf16[384,192]{0,1:T(8,128)(2,1)S(1)} %collective-permute-done.4), channel_id=1, source_target_pairs={{0,14},{2,0},{4,2},{6,4},{8,6},{10,8},{12,10},{14,12},{1,15},{3,1}... | collective-permute-start | bytes 442376 | tf_op jit(solution)/shard_map/ppermute | solution.py:18
  63.1 2.1 collective-permute-done.5
  65.2 5.2 %collective-permute-start.6 = (bf16[384,192]{0,1:T(8,128)(2,1)S(1)}, bf16[384,192]{0,1:T(8,128)(2,1)S(1)}, u32[]{:S(2)}, u32[]{:S(2)}) collective-permute-start(bf16[384,192]{0,1:T(8,128)(2,1)S(1)} %collective-permute-done.5), channel_id=1, source_target_pairs={{0,14},{2,0},{4,2},{6,4},{8,6},{10,8},{12,10},{14,12},{1,15},{3,1}... | collective-permute-start | bytes 442376 | tf_op jit(solution)/shard_map/ppermute | solution.py:18
  79.2 1.8 convolution_convert_fusion.3
  81.0 17.8 %all_gather.28 = bf16[768,384]{1,0:T(8,128)(2,1)S(1)} all-gather(bf16[192,384]{1,0:T(8,128)(2,1)S(1)} %convolution_convert_fusion.3), channel_id=1, replica_groups=mesh['groups'=2,'frames'=4,'fsdp'=2,'heads'=2] {'frames'}, dimensions={0}, use_global_device_ids=true | all-gather | bytes 737280 | tf_op jit(solution)/shard_map/all_gather | solution.py:73
  99.0 3.8 %all-gather.10.cloned.1.call-done = bf16[1536,384]{1,0:T(8,128)(2,1)} async-done(((bf16[192,384]{1,0:T(8,128)(2,1)}), bf16[1536,384]{1,0:T(8,128)(2,1)}) %all-gather.10.cloned.1.call-update) | async-done | bytes 1179664 | tf_op jit(solution)/shard_map/all_gather | solution.py:57
  102.9 1.8 convolution_convert_fusion.2
  105.5 1.5 bitcast_reduce_fusion
  107.0 38.9 %all-gather.6.cloned.1.call-done = bf16[1536,384]{1,0:T(8,128)(2,1)} async-done(((bf16[192,384]{1,0:T(8,128)(2,1)}), bf16[1536,384]{1,0:T(8,128)(2,1)}) %all-gather.6.cloned.1.call-update) | async-done | bytes 1179664 | tf_op jit(solution)/shard_map/all_gather | solution.py:59
  145.9 1.8 convolution_convert_fusion.4
  147.7 16.3 %all_gather.26 = bf16[768,384]{1,0:T(8,128)(2,1)S(1)} all-gather(bf16[192,384]{1,0:T(8,128)(2,1)S(1)} %convolution_convert_fusion.4), channel_id=1, replica_groups=mesh['groups'=2,'frames'=4,'fsdp'=2,'heads'=2] {'frames'}, dimensions={0}, use_global_device_ids=true | all-gather | bytes 737280 | tf_op jit(solution)/shard_map/all_gather | solution.py:74
  166.9 2.8 convolution_convert_fusion.1
  169.9 1.8 copy.17
  172.6 15.0 %all-reduce.2.cloned.1.call-done = bf16[192,1536]{1,0:T(8,128)(2,1)} async-done(((bf16[192,1536]{1,0:T(8,128)(2,1)}), bf16[192,1536]{1,0:T(8,128)(2,1)}) %all-reduce.2.cloned.1.call-update) | async-done | bytes 589840 | tf_op jit(solution)/shard_map/psum | solution.py:95
  189.2 44.1 %all-gather.12.cloned.1.call-done = bf16[1536,2,768]{2,0,1:T(8,128)(2,1)} async-done(((bf16[768,2,768]{2,0,1:T(8,128)(2,1)}), bf16[1536,2,768]{2,0,1:T(8,128)(2,1)}) %all-gather.12.cloned.1.call-update) | async-done | bytes 4718608 | tf_op jit(solution)/shard_map/all_gather | solution.py:104
  233.3 3.5 %fusion.27 = f32[192,2,768]{2,0,1:T(8,128)S(1)} fusion(bf16[1536,2,768]{2,0,1:T(8,128)(2,1)} %all-gather.12.cloned.1.call-done, bf16[192,1536]{1,0:T(8,128)(2,1)S(1)} %get-tuple-element.37, f32[192]{0:T(256)S(1)} %add_rsqrt_fusion, f32[192]{0:T(256)S(1)} %broadcast_multiply_fusion), kind=kOutput, calls=%fused_computation.65 | convolution fusion | flops 907149312 | bytes 6489600 | tf_op jit(solution)/shard_map/td,dgc->tgc/dot_general | solution.py:101
  237.0 3.4 %collective-permute-start.7 = (bf16[15,768]{1,0:T(8,128)(2,1)S(1)}, bf16[15,768]{1,0:T(8,128)(2,1)S(1)}, u32[]{:S(2)}, u32[]{:S(2)}) collective-permute-start(bf16[15,768]{1,0:T(8,128)(2,1)S(1)} %get-tuple-element.38), channel_id=1, source_target_pairs={{0,4},{4,8},{8,12},{1,5},{5,9},{9,13},{2,6},{6,10},{10,14},{3,7},{... | collective-permute-start | bytes 69128 | tf_op jit(solution)/shard_map/ppermute | solution.py:32
  240.4 1.5 collective-permute-start.8
  242.0 28.7 %all-gather.14.cloned.1.call-done = bf16[768,1536]{1,0:T(8,128)(2,1)} async-done(((bf16[768,768]{1,0:T(8,128)(2,1)}), bf16[768,1536]{1,0:T(8,128)(2,1)}) %all-gather.14.cloned.1.call-update) | async-done | bytes 2359312 | tf_op jit(solution)/shard_map/all_gather | solution.py:120
  270.7 5.5 %convolution_convert_fusion = bf16[192,1536]{1,0:T(8,128)(2,1)} fusion(bf16[768,1536]{1,0:T(8,128)(2,1)} %all-gather.14.cloned.1.call-done, bf16[192,768]{1,0:T(8,128)(2,1)S(1)} %fusion.37, bf16[15,768]{1,0:T(8,128)(2,1)S(1)} %collective-permute-done.8, bf16[15,768]{1,0:T(8,128)(2,1)S(1)} %collective-permute-done.7, f32[768]{0:T(1024)S(1)} %get-tuple-element.34, ...), kind=kOutput, calls=%fused_computation | convolution fusion | flops 480854016 | bytes 3385344 | tf_op jit(solution)/shard_map/dot_general | solution.py:119
  276.1 8.1 %reduce-scatter.2.cloned.1.call-done = bf16[192,768]{1,0:T(8,128)(2,1)} async-done(((bf16[192,1536]{1,0:T(8,128)(2,1)}), bf16[192,768]{1,0:T(8,128)(2,1)}) %reduce-scatter.2.cloned.1.call-update) | async-done | bytes 294928 | tf_op jit(solution)/shard_map/reduce_scatter | solution.py:122
  284.3 1.7 fusion.38
  (63 shorter events, 21.2 us)
Async XLA Ops:
  7.4 33.5 %copy-start.2 = (bf16[384,192]{0,1:T(8,128)(2,1)S(1)}, bf16[384,192]{0,1:T(8,128)(2,1)}, u32[]{:S(2)}) copy-start(bf16[384,192]{0,1:T(8,128)(2,1)} %param.14) | copy-start | bytes 442372
  7.4 71.8 %all-gather.8.cloned.1.call-start = ((), (), s32[]{:S(2)}) async-start(), calls=%async_computation.2 | async-start | bytes 1327104 | tf_op jit(solution)/shard_map/all_gather | solution.py:58
  8.1 94.8 %all-gather.10.cloned.1.call-start = ((), (), s32[]{:S(2)}) async-start(), calls=%async_computation.3 | async-start | bytes 1327104 | tf_op jit(solution)/shard_map/all_gather | solution.py:57
  8.8 137.0 %all-gather.6.cloned.1.call-start = ((), (), s32[]{:S(2)}) async-start(), calls=%async_computation.1 | async-start | bytes 1327104 | tf_op jit(solution)/shard_map/all_gather | solution.py:59
  8.9 9.5 %collective-permute-start = (bf16[384,192]{0,1:T(8,128)(2,1)}, bf16[384,192]{0,1:T(8,128)(2,1)S(1)}, u32[]{:S(2)}, u32[]{:S(2)}) collective-permute-start(bf16[384,192]{0,1:T(8,128)(2,1)} %param.14), channel_id=1, source_target_pairs={{0,14},{2,0},{4,2},{6,4},{8,6},{10,8},{12,10},{14,12},{1,15},{3,1}... | collective-permute-start | bytes 442376 | tf_op jit(solution)/shard_map/ppermute | solution.py:18
  15.0 172.6 %all-reduce.2.cloned.1.call-start = ((), (), s32[]{:S(2)}) async-start(), calls=%async_computation.4 | async-start | bytes 1179648 | tf_op jit(solution)/shard_map/psum | solution.py:95
  18.4 9.5 %collective-permute-start.1 = (bf16[384,192]{0,1:T(8,128)(2,1)S(1)}, bf16[384,192]{0,1:T(8,128)(2,1)S(1)}, u32[]{:S(2)}, u32[]{:S(2)}) collective-permute-start(bf16[384,192]{0,1:T(8,128)(2,1)S(1)} %collective-permute-done), channel_id=1, source_target_pairs={{0,14},{2,0},{4,2},{6,4},{8,6},{10,8},{12,10},{14,12},{1,15},{3,1}... | collective-permute-start | bytes 442376 | tf_op jit(solution)/shard_map/ppermute | solution.py:18
  27.9 7.9 %collective-permute-start.2 = (bf16[384,192]{0,1:T(8,128)(2,1)S(1)}, bf16[384,192]{0,1:T(8,128)(2,1)S(1)}, u32[]{:S(2)}, u32[]{:S(2)}) collective-permute-start(bf16[384,192]{0,1:T(8,128)(2,1)S(1)} %collective-permute-done.1), channel_id=1, source_target_pairs={{0,14},{2,0},{4,2},{6,4},{8,6},{10,8},{12,10},{14,12},{1,15},{3,1}... | collective-permute-start | bytes 442376 | tf_op jit(solution)/shard_map/ppermute | solution.py:18
  35.7 10.8 %collective-permute-start.3 = (bf16[384,192]{0,1:T(8,128)(2,1)S(1)}, bf16[384,192]{0,1:T(8,128)(2,1)S(1)}, u32[]{:S(2)}, u32[]{:S(2)}) collective-permute-start(bf16[384,192]{0,1:T(8,128)(2,1)S(1)} %collective-permute-done.2), channel_id=1, source_target_pairs={{0,14},{2,0},{4,2},{6,4},{8,6},{10,8},{12,10},{14,12},{1,15},{3,1}... | collective-permute-start | bytes 442376 | tf_op jit(solution)/shard_map/ppermute | solution.py:18
  46.5 10.0 %collective-permute-start.4 = (bf16[384,192]{0,1:T(8,128)(2,1)S(1)}, bf16[384,192]{0,1:T(8,128)(2,1)S(1)}, u32[]{:S(2)}, u32[]{:S(2)}) collective-permute-start(bf16[384,192]{0,1:T(8,128)(2,1)S(1)} %collective-permute-done.3), channel_id=1, source_target_pairs={{0,14},{2,0},{4,2},{6,4},{8,6},{10,8},{12,10},{14,12},{1,15},{3,1}... | collective-permute-start | bytes 442376 | tf_op jit(solution)/shard_map/ppermute | solution.py:18
  56.5 8.7 %collective-permute-start.5 = (bf16[384,192]{0,1:T(8,128)(2,1)S(1)}, bf16[384,192]{0,1:T(8,128)(2,1)S(1)}, u32[]{:S(2)}, u32[]{:S(2)}) collective-permute-start(bf16[384,192]{0,1:T(8,128)(2,1)S(1)} %collective-permute-done.4), channel_id=1, source_target_pairs={{0,14},{2,0},{4,2},{6,4},{8,6},{10,8},{12,10},{14,12},{1,15},{3,1}... | collective-permute-start | bytes 442376 | tf_op jit(solution)/shard_map/ppermute | solution.py:18
  65.2 7.9 %collective-permute-start.6 = (bf16[384,192]{0,1:T(8,128)(2,1)S(1)}, bf16[384,192]{0,1:T(8,128)(2,1)S(1)}, u32[]{:S(2)}, u32[]{:S(2)}) collective-permute-start(bf16[384,192]{0,1:T(8,128)(2,1)S(1)} %collective-permute-done.5), channel_id=1, source_target_pairs={{0,14},{2,0},{4,2},{6,4},{8,6},{10,8},{12,10},{14,12},{1,15},{3,1}... | collective-permute-start | bytes 442376 | tf_op jit(solution)/shard_map/ppermute | solution.py:18
  165.1 1.1 copy-start.1
  166.9 2.9 %copy-start = (bf16[768,2,768]{2,1,0:T(2,128)(2,1)S(1)}, bf16[768,2,768]{2,1,0:T(2,128)(2,1)}, u32[]{:S(2)}) copy-start(bf16[768,2,768]{2,1,0:T(2,128)(2,1)} %param.15) | copy-start | bytes 7077892
  169.8 63.5 %all-gather.12.cloned.1.call-start = ((), (), s32[]{:S(2)}) async-start(), calls=%async_computation.5 | async-start | bytes 7077888 | tf_op jit(solution)/shard_map/all_gather | solution.py:104
  171.6 0.8 copy-start.3
  171.7 99.0 %all-gather.14.cloned.1.call-start = ((), (), s32[]{:S(2)}) async-start(), calls=%async_computation.6 | async-start | bytes 3538944 | tf_op jit(solution)/shard_map/all_gather | solution.py:120
  172.2 112.0 %reduce-scatter.2.cloned.1.call-start = ((), (), s32[]{:S(2)}) async-start(), calls=%async_computation.7 | async-start | bytes 884736 | tf_op jit(solution)/shard_map/reduce_scatter | solution.py:122
  237.0 33.7 %collective-permute-start.7 = (bf16[15,768]{1,0:T(8,128)(2,1)S(1)}, bf16[15,768]{1,0:T(8,128)(2,1)S(1)}, u32[]{:S(2)}, u32[]{:S(2)}) collective-permute-start(bf16[15,768]{1,0:T(8,128)(2,1)S(1)} %get-tuple-element.38), channel_id=1, source_target_pairs={{0,4},{4,8},{8,12},{1,5},{5,9},{9,13},{2,6},{6,10},{10,14},{3,7},{... | collective-permute-start | bytes 69128 | tf_op jit(solution)/shard_map/ppermute | solution.py:32
  240.4 30.3 %collective-permute-start.8 = (bf16[15,768]{1,0:T(8,128)(2,1)S(1)}, bf16[15,768]{1,0:T(8,128)(2,1)S(1)}, u32[]{:S(2)}, u32[]{:S(2)}) collective-permute-start(bf16[15,768]{1,0:T(8,128)(2,1)S(1)} %get-tuple-element.39), channel_id=1, source_target_pairs={{4,0},{8,4},{12,8},{5,1},{9,5},{13,9},{6,2},{10,6},{14,10},{7,3},{... | collective-permute-start | bytes 69128 | tf_op jit(solution)/shard_map/ppermute | solution.py:34
Sparse Core Ops, SparseCore 0:
  10.3 48.8 all-gather.7
  61.4 41.4 all-gather.9
  105.0 40.7 all-gather.5
  169.9 17.6 all-reduce.1
  276.3 7.9 reduce-scatter.1
Sparse Core Ops, SparseCore 1:
  171.8 61.4 all-gather.11
  234.7 35.9 all-gather.13
